TPU v7x, 32 devices: a whole 2x2x4 slice. The times are simulated.
32 devices in a mesh: ctx: 8 (over y, x, core), fsdp: 4 (over z).
Axes of the slice: x: 2, y: 2, z: 4, core: 2. Of those that a mesh axis runs over, the one named last changes fastest.
Arguments:
- tokens: bfloat16 [4, 4096, 768], P('fsdp', 'ctx'), may hold values from -6 to 6
- cotangent: bfloat16 [4, 4096, 768], P('fsdp', 'ctx'), may hold values from -6 to 6
- lengths: int32 [4, 4], P('fsdp'), may hold values from 1 to 2048, 4096 in all within a row
- dealing: int32 [4, 16], P('fsdp'), may hold values from 0 to 15, each once within a row
- qkv_weight: bfloat16 [768, 2304], P('fsdp'), may hold values from -0.21875 to 0.21875
- out_weight: bfloat16 [768, 768], P('fsdp'), may hold values from -0.21875 to 0.21875
- in_weight: bfloat16 [768, 3072], P('fsdp'), may hold values from -0.21875 to 0.21875
- back_weight: bfloat16 [3072, 768], P('fsdp'), may hold values from -0.109375 to 0.109375
- norm_gains: bfloat16 [3, 768], P(None, 'fsdp'), may hold values from 0.25 to 1.75
- shifts: bfloat16 [7, 768], P(None, 'fsdp'), may hold values from -1.796875 to 1.796875
- ffn_gain: bfloat16 [3072], P('fsdp'), may hold values from 0.25 to 1.75
- ffn_shifts: bfloat16 [2, 3072], P(None, 'fsdp'), may hold values from -1.796875 to 1.796875
Outputs:
- mixed_out: bfloat16 [4, 4096, 768], P('fsdp', 'ctx')
- input_grad: float32 [4, 4096, 768], P('fsdp', 'ctx')
- qkv_grad: float32 [768, 2304], P(('ctx', 'fsdp'))
- out_grad: float32 [768, 768], P(('ctx', 'fsdp'))
- in_grad: float32 [768, 3072], P(('ctx', 'fsdp'))
- back_grad: float32 [3072, 768], P(('ctx', 'fsdp'))
- gains_grad: float32 [3, 768], P(None, ('ctx', 'fsdp'))
- shifts_grad: float32 [7, 768], P(None, ('ctx', 'fsdp'))
- ffn_gain_grad: float32 [3072], P(('ctx', 'fsdp'))
- ffn_shifts_grad: float32 [2, 3072], P(None, ('ctx', 'fsdp'))
Inputs may be any that keep to these rules, and one draw needn't show every extreme that they name: `lengths`: each row sums to 4096 and its largest entry is exactly 2048. `dealing`: each row is a permutation of the group numbers.
All inputs are finite; a program needn't handle non-finite values.
Results may differ from a plain program's by a relative error of at most 0.018.
Values may be sent and summed in bfloat16 or wider, within the bound.
No kernel may reach another device: no remote copies, remote signals or barrier semaphores. Data moves between devices by JAX's collectives and lax.ppermute only.
A program may use at most 256 MiB of HBM per device.

v0:
```python
import math
import jax
import jax.numpy as jnp
from jax import lax
from jax.sharding import PartitionSpec as P

D = 768
H = 12
DH = 64


def layer_norm(values, gain, shift):
    average = jnp.mean(values, axis=-1, keepdims=True)
    centred = values - average
    variance = jnp.mean(centred * centred, axis=-1, keepdims=True)
    return centred * lax.rsqrt(variance + 1e-05) * gain + shift


def gelu_exact(values):
    return jax.nn.gelu(values, approximate=False)


def row_places(first_row, row_count, deal_row, bounds, group_rows):
    row_ids = first_row + jnp.arange(row_count, dtype=jnp.int32)
    group_ids = row_ids // group_rows
    onehot = (group_ids[:, None] == jnp.arange(deal_row.shape[0], dtype=jnp.int32)[None, :]).astype(
        jnp.int32
    )
    picked = jnp.sum(onehot * deal_row[None, :], axis=1)
    places = picked * group_rows + row_ids % group_rows
    segment = jnp.sum((places[:, None] >= bounds[None, :]).astype(jnp.int32), axis=1)
    return (places, segment)


def outer_sum(left, right):
    return lax.dot_general(
        left, right, (((0,), (0,)), ((), ())), preferred_element_type=jnp.float32
    )


def times_transposed(left, matrix):
    return lax.dot_general(
        left, matrix, (((1,), (1,)), ((), ())), preferred_element_type=jnp.float32
    )


def unpack(loaded):
    qkv_w, out_w, in_w, back_w, gains, shift_rows, ffn_gain, ffn_shift_rows = loaded
    return (
        qkv_w,
        out_w,
        in_w,
        back_w,
        gains.astype(jnp.float32),
        shift_rows.astype(jnp.float32),
        ffn_gain.astype(jnp.float32),
        ffn_shift_rows.astype(jnp.float32),
    )


def local(
    tokens,
    cotangent,
    lengths,
    dealing,
    qkv_weight,
    out_weight,
    in_weight,
    back_weight,
    norm_gains,
    shifts,
    ffn_gain,
    ffn_shifts,
):
    position = lax.axis_index("ctx")
    tok_rows = tokens.shape[1]
    group_rows = tok_rows // 2
    deal_row = dealing[0]
    bounds = jnp.cumsum(lengths[0])
    scaling = DH ** (-0.5)
    loaded = (
        lax.all_gather(qkv_weight, "fsdp", axis=0, tiled=True),
        lax.all_gather(out_weight, "fsdp", axis=0, tiled=True),
        lax.all_gather(in_weight, "fsdp", axis=0, tiled=True),
        lax.all_gather(back_weight, "fsdp", axis=0, tiled=True),
        lax.all_gather(norm_gains, "fsdp", axis=1, tiled=True),
        lax.all_gather(shifts, "fsdp", axis=1, tiled=True),
        lax.all_gather(ffn_gain, "fsdp", axis=0, tiled=True),
        lax.all_gather(ffn_shifts, "fsdp", axis=1, tiled=True),
    )
    qkv_w, out_w, in_w, back_w, gains, shift_rows, ffn_scale, ffn_shift_rows = unpack(loaded)
    inputs = tokens[0].astype(jnp.float32)
    normed = layer_norm(inputs, gains[0], shift_rows[0])
    normed_low = normed.astype(jnp.bfloat16)
    projected = jnp.dot(normed_low, qkv_w, preferred_element_type=jnp.float32)
    query = (projected[:, :D] + shift_rows[1]).astype(jnp.bfloat16)
    keyed = projected[:, D : 2 * D].astype(jnp.bfloat16)
    valued = (projected[:, 2 * D :] + shift_rows[2]).astype(jnp.bfloat16)
    query3 = query.reshape(tok_rows, H, DH)
    q_places, q_segment = row_places(position * tok_rows, tok_rows, deal_row, bounds, group_rows)

    def allowed_pairs(qp, qs, k_places, k_segment):
        return ((k_segment[None, :] == qs[:, None]) & (k_places[None, :] <= qp[:, None]))[None]

    initial = (
        jnp.full((H, tok_rows), -1e30, jnp.float32),
        jnp.zeros((H, tok_rows), jnp.float32),
        jnp.zeros((H, tok_rows, DH), jnp.float32),
    )
    key_rows = lax.all_gather(keyed, "ctx", axis=0, tiled=True)
    value_rows = lax.all_gather(valued, "ctx", axis=0, tiled=True)
    key_count = key_rows.shape[0]
    block_rows = 512
    block_count = key_count // block_rows
    k_places, k_segment = row_places(jnp.int32(0), key_count, deal_row, bounds, group_rows)
    stacked = (
        key_rows.reshape(block_count, block_rows, H, DH),
        value_rows.reshape(block_count, block_rows, H, DH),
        k_places.reshape(block_count, block_rows),
        k_segment.reshape(block_count, block_rows),
    )

    def visit_block(inner_state, pieces):
        maxima, totals, weighted = inner_state
        key3, value3, block_places, block_segment = pieces
        scores = (
            jnp.einsum("qhd,khd->hqk", query3, key3, preferred_element_type=jnp.float32) * scaling
        )
        allowed = allowed_pairs(q_places, q_segment, block_places, block_segment)
        masked = jnp.where(allowed, scores, -1e30)
        raised = jnp.maximum(maxima, jnp.max(masked, axis=-1))
        rescale = jnp.exp(maxima - raised)
        expo = jnp.where(allowed, jnp.exp(masked - raised[..., None]), 0.0)
        totals = totals * rescale + jnp.sum(expo, axis=-1)
        weighted = weighted * rescale[..., None] + jnp.einsum(
            "hqk,khd->hqd", expo.astype(jnp.bfloat16), value3, preferred_element_type=jnp.float32
        )
        return ((raised, totals, weighted), None)

    maxima, totals, weighted = lax.scan(visit_block, initial, stacked)[0]
    context3 = weighted / totals[..., None]
    log_total = maxima + jnp.log(totals)
    context = context3.transpose(1, 0, 2).reshape(tok_rows, D)
    inner = layer_norm(context, gains[1], shift_rows[3])
    inner_low = inner.astype(jnp.bfloat16)
    branch = jnp.dot(inner_low, out_w, preferred_element_type=jnp.float32) + shift_rows[4]
    middle = inputs + branch
    normed_two = layer_norm(middle, gains[2], shift_rows[5])
    normed_two_low = normed_two.astype(jnp.bfloat16)
    hidden = jnp.dot(normed_two_low, in_w, preferred_element_type=jnp.float32) + ffn_shift_rows[0]
    activated = gelu_exact(hidden)
    inner_two = layer_norm(activated, ffn_scale, ffn_shift_rows[1])
    inner_two_low = inner_two.astype(jnp.bfloat16)
    result = jnp.dot(inner_two_low, back_w, preferred_element_type=jnp.float32) + shift_rows[6]
    mixed_out = (middle + result).astype(jnp.bfloat16)
    loaded_back = (
        lax.all_gather(qkv_weight, "fsdp", axis=0, tiled=True),
        lax.all_gather(out_weight, "fsdp", axis=0, tiled=True),
        lax.all_gather(in_weight, "fsdp", axis=0, tiled=True),
        lax.all_gather(back_weight, "fsdp", axis=0, tiled=True),
        lax.all_gather(norm_gains, "fsdp", axis=1, tiled=True),
        lax.all_gather(shifts, "fsdp", axis=1, tiled=True),
        lax.all_gather(ffn_gain, "fsdp", axis=0, tiled=True),
        lax.all_gather(ffn_shifts, "fsdp", axis=1, tiled=True),
    )
    qkv_w, out_w, in_w, back_w, gains, shift_rows, ffn_scale, ffn_shift_rows = unpack(loaded_back)
    upstream = cotangent[0].astype(jnp.float32)
    result_low = cotangent[0]
    grad_back_w = outer_sum(inner_two_low, result_low)
    grad_back_bias = jnp.sum(result_low.astype(jnp.float32), axis=0)
    grad_inner_two = times_transposed(result_low, back_w)
    norm_pull = jax.vjp(layer_norm, activated, ffn_scale, ffn_shift_rows[1])[1]
    grad_activated, grad_ffn_gain, grad_ffn_shift = norm_pull(grad_inner_two)
    gelu_pull = jax.vjp(gelu_exact, hidden)[1]
    grad_hidden = gelu_pull(grad_activated)[0]
    hidden_low = grad_hidden.astype(jnp.bfloat16)
    grad_in_w = outer_sum(normed_two_low, hidden_low)
    grad_in_bias = jnp.sum(hidden_low.astype(jnp.float32), axis=0)
    grad_normed_two = times_transposed(hidden_low, in_w)
    second_pull = jax.vjp(layer_norm, middle, gains[2], shift_rows[5])[1]
    grad_middle_part, grad_gain_two, grad_shift_five = second_pull(grad_normed_two)
    grad_middle = upstream + grad_middle_part
    branch_low = grad_middle.astype(jnp.bfloat16)
    grad_out_w = outer_sum(inner_low, branch_low)
    grad_out_bias = jnp.sum(branch_low.astype(jnp.float32), axis=0)
    grad_inner = times_transposed(branch_low, out_w)
    inner_pull = jax.vjp(layer_norm, context, gains[1], shift_rows[3])[1]
    grad_context, grad_gain_one, grad_shift_three = inner_pull(grad_inner)
    context_grad_low = grad_context.astype(jnp.bfloat16).reshape(tok_rows, H, DH)
    delta = jnp.einsum("qhd,hqd->hq", context_grad_low.astype(jnp.float32), context3)

    def grad_pair(
        q_rows, grad_rows, lse_rows, delta_rows, qp, qs, key3, value3, k_places, k_segment
    ):
        scores = (
            jnp.einsum("qhd,khd->hqk", q_rows, key3, preferred_element_type=jnp.float32) * scaling
        )
        allowed = allowed_pairs(qp, qs, k_places, k_segment)
        probabilities = jnp.where(allowed, jnp.exp(scores - lse_rows[..., None]), 0.0)
        upstream_probs = jnp.einsum(
            "qhd,khd->hqk", grad_rows, value3, preferred_element_type=jnp.float32
        )
        score_grad = (probabilities * (upstream_probs - delta_rows[..., None])).astype(jnp.bfloat16)
        query_add = (
            jnp.einsum("hqk,khd->qhd", score_grad, key3, preferred_element_type=jnp.float32)
            * scaling
        )
        key_add = (
            jnp.einsum("hqk,qhd->khd", score_grad, q_rows, preferred_element_type=jnp.float32)
            * scaling
        )
        value_add = jnp.einsum(
            "hqk,qhd->khd",
            probabilities.astype(jnp.bfloat16),
            grad_rows,
            preferred_element_type=jnp.float32,
        )
        return (query_add, key_add, value_add)

    def grad_block(key3, value3, k_places, k_segment):
        return grad_pair(
            query3,
            context_grad_low,
            log_total,
            delta,
            q_places,
            q_segment,
            key3,
            value3,
            k_places,
            k_segment,
        )

    zero_query = jnp.zeros((tok_rows, H, DH), jnp.float32)
    gathered_keys, gathered_values = (
        lax.all_gather(keyed, "ctx", axis=0, tiled=True),
        lax.all_gather(valued, "ctx", axis=0, tiled=True),
    )
    stream_rows = gathered_keys.shape[0]
    block_rows = math.gcd(stream_rows, 512)
    block_count = stream_rows // block_rows
    all_places, all_segment = row_places(0, stream_rows, deal_row, bounds, group_rows)

    def sweep(query_grad, pieces):
        key3, value3, block_places, block_segment = pieces
        query_add, key_add, value_add = grad_block(key3, value3, block_places, block_segment)
        return (query_grad + query_add, (key_add, value_add))

    query_grad, (key_parts, value_parts) = lax.scan(
        sweep,
        zero_query,
        (
            gathered_keys.reshape(block_count, block_rows, H, DH),
            gathered_values.reshape(block_count, block_rows, H, DH),
            all_places.reshape(block_count, block_rows),
            all_segment.reshape(block_count, block_rows),
        ),
    )
    key_terms = key_parts.reshape(stream_rows, D)
    value_terms = value_parts.reshape(stream_rows, D)
    key_grad_mine, value_grad_mine = (
        lax.psum_scatter(
            key_terms.astype(jnp.bfloat16), "ctx", scatter_dimension=0, tiled=True
        ).astype(jnp.float32),
        lax.psum_scatter(
            value_terms.astype(jnp.bfloat16), "ctx", scatter_dimension=0, tiled=True
        ).astype(jnp.float32),
    )
    qkv_grad_low = jnp.concatenate(
        [query_grad.reshape(tok_rows, D), key_grad_mine, value_grad_mine], axis=1
    ).astype(jnp.bfloat16)
    grad_qkv_w = outer_sum(normed_low, qkv_grad_low)
    column_sums = jnp.sum(qkv_grad_low.astype(jnp.float32), axis=0)
    grad_query_bias = column_sums[:D]
    grad_value_bias = column_sums[2 * D :]
    grad_normed = times_transposed(qkv_grad_low, qkv_w)
    first_pull = jax.vjp(layer_norm, inputs, gains[0], shift_rows[0])[1]
    grad_inputs_part, grad_gain_zero, grad_shift_zero = first_pull(grad_normed)
    input_grad = grad_middle + grad_inputs_part
    gains_terms = jnp.stack([grad_gain_zero, grad_gain_one, grad_gain_two])
    shift_terms = jnp.stack(
        [
            grad_shift_zero,
            grad_query_bias,
            grad_value_bias,
            grad_shift_three,
            grad_out_bias,
            grad_shift_five,
            grad_back_bias,
        ]
    )
    ffn_shift_terms = jnp.stack([grad_in_bias, grad_ffn_shift])
    reduced = (
        lax.psum_scatter(grad_qkv_w, ("ctx", "fsdp"), scatter_dimension=0, tiled=True),
        lax.psum_scatter(grad_out_w, ("ctx", "fsdp"), scatter_dimension=0, tiled=True),
        lax.psum_scatter(grad_in_w, ("ctx", "fsdp"), scatter_dimension=0, tiled=True),
        lax.psum_scatter(grad_back_w, ("ctx", "fsdp"), scatter_dimension=0, tiled=True),
        lax.psum_scatter(gains_terms, ("ctx", "fsdp"), scatter_dimension=1, tiled=True),
        lax.psum_scatter(shift_terms, ("ctx", "fsdp"), scatter_dimension=1, tiled=True),
        lax.psum_scatter(grad_ffn_gain, ("ctx", "fsdp"), scatter_dimension=0, tiled=True),
        lax.psum_scatter(ffn_shift_terms, ("ctx", "fsdp"), scatter_dimension=1, tiled=True),
    )
    return (mixed_out[None], input_grad[None]) + tuple(reduced)


def solution(mesh):
    in_specs = (
        P("fsdp", "ctx", None),
        P("fsdp", "ctx", None),
        P("fsdp", None),
        P("fsdp", None),
        P("fsdp", None),
        P("fsdp", None),
        P("fsdp", None),
        P("fsdp", None),
        P(None, "fsdp"),
        P(None, "fsdp"),
        P("fsdp"),
        P(None, "fsdp"),
    )
    out_specs = (
        P("fsdp", "ctx", None),
        P("fsdp", "ctx", None),
        P(("ctx", "fsdp"), None),
        P(("ctx", "fsdp"), None),
        P(("ctx", "fsdp"), None),
        P(("ctx", "fsdp"), None),
        P(None, ("ctx", "fsdp")),
        P(None, ("ctx", "fsdp")),
        P(("ctx", "fsdp")),
        P(None, ("ctx", "fsdp")),
    )
    return jax.shard_map(local, mesh=mesh, in_specs=in_specs, out_specs=out_specs, check_vma=False)
```

profile of v0, /device:TPU:0, one launch (start us, length us, event | category | flops | bytes accessed | tf_op | source)
XLA Modules:
  0.0 1461.5 jit_solution(8794208688010352200)
XLA Ops:
  8.0 14.9 %all-gather.1 = bf16[4,192,7]{1,2,0:T(8,128)(2,1)S(1)} all-gather(bf16[1,192,7]{1,2,0:T(8,128)(2,1)} %bitcast.267), channel_id=1, replica_groups=mesh['ctx'=8,'fsdp'=4] {'fsdp'}, dimensions={0}, use_global_device_ids=true | all-gather | bytes 13440 | tf_op jit(solution)/shard_map/all_gather | solution.py:87
  23.0 12.2 all-gather
  38.9 43.6 %all-gather.10.cloned.1.call-done = bf16[768,2304]{1,0:T(8,128)(2,1)} async-done(((bf16[192,2304]{1,0:T(8,128)(2,1)}), bf16[768,2304]{1,0:T(8,128)(2,1)}) %all-gather.10.cloned.1.call-update) | async-done | bytes 3538960 | tf_op jit(solution)/shard_map/all_gather | solution.py:82
  95.8 13.0 all_gather.45
  109.5 13.6 all-gather.2
  124.2 10.1 all-gather.12.cloned.1.call-done
  134.3 8.6 copy.91
  155.3 26.5 %all-gather.14.cloned.1.call-done = bf16[4096,768]{1,0:T(8,128)(2,1)} async-done(((bf16[512,768]{1,0:T(8,128)(2,1)}), bf16[4096,768]{1,0:T(8,128)(2,1)}) %all-gather.14.cloned.1.call-update) | async-done | bytes 6291472 | tf_op jit(solution)/shard_map/all_gather | solution.py:111
  181.8 8.9 copy.93
  202.6 179.3 %while.30 = (s32[]{:T(128)}, f32[12,512]{1,0:T(8,128)S(1)}, f32[12,512]{1,0:T(8,128)S(1)}, f32[12,512,64]{1,2,0:T(8,128)}, s32[8,512]{1,0:T(8,128)S(1)}, /*index...) while((s32[]{:T(128)}, f32[12,512]{1,0:T(8,128)S(1)}, ...), condition=%wide.region_10.11_spmd.clone, body=%wide.region_7.10_spmd.clone.sunk | while | flops 848197632 | bytes 95043760 | solution.py:140
  389.9 21.5 %fusion.101 = (f32[512]{0:T(512)S(1)}, f32[512,3072]{1,0:T(8,128)}, f32[512,3072]{1,0:T(8,128)}, f32[512,3072]{1,0:T(8,128)}) fusion(f32[3072]{0:T(1024)S(1)} %bitcast.261, bf16[768,3072]{1,0:T(8,128)(2,1)} %all-gather.18.cloned.1.call-done, f32[512,768]{1,0:T(8,128)} %copy-done.10, f32[768]{0:T(1024)S(1)} %get-tuple-element.371, ...), kind=kOutput, calls=%fused_computation.205 | convolution fusion | flops 2521693696 | bytes 25190400 | tf_op jit(solution)/shard_map/dot_general | solution.py:150
  422.2 10.8 convert_reduce_fusion
  447.7 251.0 %while.31 = (s32[]{:T(128)}, f32[512,12,64]{0,2,1:T(8,128)}, bf16[8,512,12,64]{1,3,2,0:T(8,128)(2,1)}, bf16[8,512,12,64]{1,3,2,0:T(8,128)(2,1)}, bf16[8,512,12,6...) while((s32[]{:T(128)}, f32[512,12,64]{0,2,1:T(8,128)}, ...), condition=%wide.region_24.25_spmd.clone, body=%wide.region_23.24_spmd.clone.sunk | while | flops 2047082496 | bytes 195125520 | solution.py:249
  486.7 8.4 fusion.165
  580.8 8.4 fusion.165
  612.1 8.4 fusion.165
  750.1 24.5 %reduce-scatter.14.cloned.1.call-done = bf16[512,768]{0,1:T(8,128)(2,1)} async-done(((bf16[4096,768]{0,1:T(8,128)(2,1)}), bf16[512,768]{0,1:T(8,128)(2,1)}) %reduce-scatter.14.cloned.1.call-update) | async-done | bytes 786448 | tf_op jit(solution)/shard_map/reduce_scatter | solution.py:265
  774.6 65.5 %reduce-scatter.12.cloned.1.call-done = bf16[512,768]{0,1:T(8,128)(2,1)} async-done(((bf16[4096,768]{0,1:T(8,128)(2,1)}), bf16[512,768]{0,1:T(8,128)(2,1)}) %reduce-scatter.12.cloned.1.call-update) | async-done | bytes 786448 | tf_op jit(solution)/shard_map/reduce_scatter | solution.py:262
  855.0 87.4 %reduce-scatter.24.cloned.1.call-done = f32[96,2]{1,0:T(8,128)} async-done(((f32[3072,2]{1,0:T(8,128)}), f32[96,2]{1,0:T(8,128)}) %reduce-scatter.24.cloned.1.call-update) | async-done | bytes 784
  952.3 40.7 %all-reduce.3 = (f32[3,768]{1,0:T(4,128)S(1)}, f32[7,768]{1,0:T(8,128)S(1)}, f32[3072]{0:T(1024)S(1)}) all-reduce(f32[3,768]{1,0:T(4,128)S(1)} %pad_maximum_fusion.2, f32[7,768]{1,0:T(8,128)S(1)} %stack.36, f32[3072]{0:T(1024)S(1)} %copy-done.25), channel_id=8, replica_groups=mesh['ctx'=8,'fsdp'=4] {'ctx','fsdp'}, use_global_device_ids=true, to_apply=%region_36.37.clone | all-reduce | flops 10752 | bytes 86016
  994.9 51.3 %reduce-scatter.18.cloned.1.call-done = f32[24,768]{1,0:T(8,128)} async-done(((f32[768,768]{1,0:T(8,128)}), f32[24,768]{1,0:T(8,128)}) %reduce-scatter.18.cloned.1.call-update) | async-done | bytes 73744 | tf_op jit(solution)/shard_map/reduce_scatter | solution.py:295
  1046.2 142.2 %reduce-scatter.20.cloned.1.call-done = f32[24,3072]{1,0:T(8,128)} async-done(((f32[768,3072]{1,0:T(8,128)}), f32[24,3072]{1,0:T(8,128)}) %reduce-scatter.20.cloned.1.call-update) | async-done | bytes 294928 | tf_op jit(solution)/shard_map/reduce_scatter | solution.py:296
  1188.4 140.8 %reduce-scatter.22.cloned.1.call-done = f32[96,768]{1,0:T(8,128)} async-done(((f32[3072,768]{1,0:T(8,128)}), f32[96,768]{1,0:T(8,128)}) %reduce-scatter.22.cloned.1.call-update) | async-done | bytes 294928 | tf_op jit(solution)/shard_map/reduce_scatter | solution.py:297
  1329.2 125.6 %reduce-scatter.16.cloned.1.call-done = f32[24,2304]{1,0:T(8,128)} async-done(((f32[768,2304]{1,0:T(8,128)}), f32[24,2304]{1,0:T(8,128)}) %reduce-scatter.16.cloned.1.call-update) | async-done | bytes 221200 | tf_op jit(solution)/shard_map/reduce_scatter | solution.py:294
  (411 shorter events, 558.4 us)
Async XLA Ops:
  7.2 75.3 %all-gather.10.cloned.1.call-start = ((), (), s32[]{:S(2)}) async-start(), calls=%async_computation.7 | async-start | bytes 4423680 | tf_op jit(solution)/shard_map/all_gather | solution.py:82
  7.9 126.4 %all-gather.12.cloned.1.call-start = ((), (), s32[]{:S(2)}) async-start(), calls=%async_computation.8 | async-start | bytes 7077888 | tf_op jit(solution)/shard_map/all_gather | solution.py:110
  35.4 51.5 %copy-start.26 = (f32[768]{0:T(1024)}, f32[768]{0:T(1024)S(1)}, u32[]{:S(2)}) copy-start(f32[768]{0:T(1024)S(1)} %get-tuple-element.379) | copy-start | bytes 9220
  36.0 50.9 %copy-start.39 = (f32[768]{0:T(1024)}, f32[768]{0:T(1024)S(1)}, u32[]{:S(2)}) copy-start(f32[768]{0:T(1024)S(1)} %get-tuple-element.376) | copy-start | bytes 9220
  36.0 349.6 %copy-start.43 = (f32[768]{0:T(1024)}, f32[768]{0:T(1024)S(1)}, u32[]{:S(2)}) copy-start(f32[768]{0:T(1024)S(1)} %get-tuple-element.373) | copy-start | bytes 9220
  36.0 353.9 %copy-start.41 = (f32[768]{0:T(1024)}, f32[768]{0:T(1024)S(1)}, u32[]{:S(2)}) copy-start(f32[768]{0:T(1024)S(1)} %get-tuple-element.371) | copy-start | bytes 9220
  37.3 49.5 %copy-start.28 = (f32[512]{0:T(512)}, f32[512]{0:T(512)S(1)}, u32[]{:S(2)}) copy-start(f32[512]{0:T(512)S(1)} %broadcast_multiply_fusion.4) | copy-start | bytes 6148
  38.8 48.0 %copy-start.32 = (f32[512]{0:T(512)}, f32[512]{0:T(512)S(1)}, u32[]{:S(2)}) copy-start(f32[512]{0:T(512)S(1)} %fusion.57) | copy-start | bytes 6148
  90.1 91.7 %all-gather.14.cloned.1.call-start = ((), (), s32[]{:S(2)}) async-start(), calls=%async_computation.9 | async-start | bytes 7077888 | tf_op jit(solution)/shard_map/all_gather | solution.py:111
  93.2 292.3 %all-gather.16.cloned.1.call-start = ((), (), s32[]{:S(2)}) async-start(), calls=%async_computation.10 | async-start | bytes 1474560 | tf_op jit(solution)/shard_map/all_gather | solution.py:83
  93.8 296.1 %all-gather.18.cloned.1.call-start = ((), (), s32[]{:S(2)}) async-start(), calls=%async_computation.11 | async-start | bytes 5898240 | tf_op jit(solution)/shard_map/all_gather | solution.py:84
  94.4 317.0 %all-gather.20.cloned.1.call-start = ((), (), s32[]{:S(2)}) async-start(), calls=%async_computation.12 | async-start | bytes 5898240 | tf_op jit(solution)/shard_map/all_gather | solution.py:85
  94.9 679.7 %reduce-scatter.14.cloned.1.call-start = ((), (), s32[]{:S(2)}) async-start(), calls=%async_computation.14 | async-start | bytes 7077888 | tf_op jit(solution)/shard_map/reduce_scatter | solution.py:265
  712.4 127.7 %reduce-scatter.12.cloned.1.call-start = ((), (), s32[]{:S(2)}) async-start(), calls=%async_computation.13 | async-start | bytes 7077888 | tf_op jit(solution)/shard_map/reduce_scatter | solution.py:262
  727.0 215.4 %reduce-scatter.24.cloned.1.call-start = ((), (), s32[]{:S(2)}) async-start(), calls=%async_computation.19 | async-start | bytes 1622016
  729.4 316.8 %reduce-scatter.18.cloned.1.call-start = ((), (), s32[]{:S(2)}) async-start(), calls=%async_computation.16 | async-start | bytes 2433024 | tf_op jit(solution)/shard_map/reduce_scatter | solution.py:295
  733.2 455.3 %reduce-scatter.20.cloned.1.call-start = ((), (), s32[]{:S(2)}) async-start(), calls=%async_computation.17 | async-start | bytes 9732096 | tf_op jit(solution)/shard_map/reduce_scatter | solution.py:296
  740.5 588.7 %reduce-scatter.22.cloned.1.call-start = ((), (), s32[]{:S(2)}) async-start(), calls=%async_computation.18 | async-start | bytes 9732096 | tf_op jit(solution)/shard_map/reduce_scatter | solution.py:297
  748.6 91.6 %copy-start.9 = (bf16[1,512,768]{2,1,0:T(8,128)(2,1)S(1)}, bf16[1,512,768]{2,1,0:T(8,128)(2,1)}, u32[]{:S(2)}) copy-start(bf16[1,512,768]{2,1,0:T(8,128)(2,1)} %param.16) | copy-start | bytes 2359300
  748.6 91.6 %copy-start.27 = (f32[768]{0:T(1024)S(1)}, f32[768]{0:T(1024)}, u32[]{:S(2)}) copy-start(f32[768]{0:T(1024)} %copy-done.26) | copy-start | bytes 9220
  748.6 91.6 %copy-start.29 = (f32[512]{0:T(512)S(1)}, f32[512]{0:T(512)}, u32[]{:S(2)}) copy-start(f32[512]{0:T(512)} %copy-done.28) | copy-start | bytes 6148
  748.6 91.6 %copy-start.31 = (f32[512]{0:T(512)S(1)}, f32[512]{0:T(512)}, u32[]{:S(2)}) copy-start(f32[512]{0:T(512)} %copy-done.30) | copy-start | bytes 6148
  748.6 91.6 %copy-start.40 = (f32[768]{0:T(1024)S(1)}, f32[768]{0:T(1024)}, u32[]{:S(2)}) copy-start(f32[768]{0:T(1024)} %copy-done.39) | copy-start | bytes 9220
  748.6 706.2 %reduce-scatter.16.cloned.1.call-start = ((), (), s32[]{:S(2)}) async-start(), calls=%async_computation.15 | async-start | bytes 7299072 | tf_op jit(solution)/shard_map/reduce_scatter | solution.py:294
  (71 other events, 431.7 us)
Sparse Core Ops, SparseCore 0:
  9.6 72.8 all-gather.9
  90.2 44.0 all-gather.11
  136.2 45.5 all-gather.13
  183.2 30.4 all-gather.15
  215.1 88.5 all-gather.17
  305.1 87.8 all-gather.19
  712.5 62.0 reduce-scatter.13
  778.4 61.7 reduce-scatter.11
  845.4 96.9 reduce-scatter.23
  948.1 98.0 reduce-scatter.17
  1053.7 134.6 reduce-scatter.19
  1194.8 134.4 reduce-scatter.21
  1336.4 118.3 reduce-scatter.15
where the time goes:
time: 1470 us; the launch traced here: 1460 us
  waiting for transfers between devices  720 us (49%)
  matrix products  403 us (27%)
  local copies, waits for them, and re-layouts  131 us (9%)
  other arithmetic  96.1 us (7%)
  blocking collectives  94.5 us (6%)
  between operations  14.9 us (1%)
    reduce_scatter x1, waiting for transfers between devices, local(): lax.psum_scatter(grad_in_w, ('ctx', 'fsdp'), scatter_dimension=0, tiled=T...  142 us
    reduce_scatter x1, waiting for transfers between devices, local(): lax.psum_scatter(grad_back_w, ('ctx', 'fsdp'), scatter_dimension=0, tiled...  141 us
    reduce_scatter x1, waiting for transfers between devices, local(): lax.psum_scatter(grad_qkv_w, ('ctx', 'fsdp'), scatter_dimension=0, tiled=...  126 us
    unnamed x14, waiting for transfers between devices  89.8 us
    dot_general x8, matrix products, grad_pair(): jnp.einsum('qhd,khd->hqk', grad_rows, value3, preferred_element_type=jnp....  67.5 us
    reduce_scatter x1, waiting for transfers between devices, local(): lax.psum_scatter(key_terms.astype(jnp.bfloat16), 'ctx', scatter_dimension...  65.5 us
    dot_general x8, matrix products, visit_block(): jnp.einsum('qhd,khd->hqk', query3, key3, preferred_element_type=jnp.float32)  64 us
    reduce_sum x8, other arithmetic, visit_block(): totals = totals * rescale + jnp.sum(expo, axis=-1)  61.3 us
  transfers between devices with their start and end apart: 13, of which 10 were waited for; matrix products, arithmetic and copies ran while one was open for 21% of the time, Pallas kernels for 0%

commit v1 on v0

--- a/solution.py
+++ b/solution.py
@@ -108,7 +108,13 @@
         jnp.zeros((H, tok_rows, DH), jnp.float32),
     )
     key_rows = lax.all_gather(keyed, "ctx", axis=0, tiled=True)
-    value_rows = lax.all_gather(valued, "ctx", axis=0, tiled=True)
+    devices = lax.axis_size("ctx")
+    current, blocks = (valued, [valued])
+    for _ in range(devices - 1):
+        current = lax.ppermute(current, "ctx", [(i, (i + 1) % devices) for i in range(devices)])
+        blocks.insert(0, current)
+    line = jnp.concatenate(blocks, axis=0)
+    value_rows = jnp.roll(line, (lax.axis_index("ctx") + 1) * valued.shape[0], axis=0)
     key_count = key_rows.shape[0]
     block_rows = 512
     block_count = key_count // block_rows

time: 1470 us -> 1560 us (1.061)
  waiting for transfers between devices: 720 us -> 777 us
  local copies, waits for them, and re-layouts: 131 us -> 163 us
    ppermute x0 -> x7, waiting for transfers between devices: none -> 94.1 us  [local(): lax.ppermute(current, 'ctx', [(i, (i + 1) % devices) for i in range(devic...]
    all_gather x1, waiting for transfers between devices: 26.5 us -> 0.02 us  [local(): lax.all_gather(valued, 'ctx', axis=0, tiled=True)]
    unnamed x112 -> x145, local copies, waits for them, and re-layouts: 54 us -> 73.4 us
  transfers between devices with their start and end apart: 13 -> 20, of which waited for: 10 -> 14; matrix products, arithmetic and copies ran while one was open for 21% -> 21% of each run, Pallas kernels for 0% -> 0%
where the time goes in v1:
time: 1560 us; the launch traced here: 1550 us
  waiting for transfers between devices  777 us (50%)
  matrix products  404 us (26%)
  local copies, waits for them, and re-layouts  163 us (10%)
  other arithmetic  96.3 us (6%)
  blocking collectives  94.6 us (6%)
    reduce_scatter x1, waiting for transfers between devices, local(): lax.psum_scatter(grad_in_w, ('ctx', 'fsdp'), scatter_dimension=0, tiled=T...  142 us
    reduce_scatter x1, waiting for transfers between devices, local(): lax.psum_scatter(grad_back_w, ('ctx', 'fsdp'), scatter_dimension=0, tiled...  141 us
    reduce_scatter x1, waiting for transfers between devices, local(): lax.psum_scatter(grad_qkv_w, ('ctx', 'fsdp'), scatter_dimension=0, tiled=...  125 us
    ppermute x7, waiting for transfers between devices, local(): lax.ppermute(current, 'ctx', [(i, (i + 1) % devices) for i in range(devic...  94.1 us
    unnamed x14, waiting for transfers between devices  90 us
    unnamed x145, local copies, waits for them, and re-layouts  73.4 us
    dot_general x8, matrix products, grad_pair(): jnp.einsum('qhd,khd->hqk', grad_rows, value3, preferred_element_type=jnp....  67.5 us
    reduce_scatter x1, waiting for transfers between devices, local(): lax.psum_scatter(key_terms.astype(jnp.bfloat16), 'ctx', scatter_dimension...  65.5 us
  transfers between devices with their start and end apart: 20, of which 14 were waited for; matrix products, arithmetic and copies ran while one was open for 21% of the time, Pallas kernels for 0%

profile of v1, /device:TPU:0, one launch (start us, length us, event | category | flops | bytes accessed | tf_op | source)
XLA Modules:
  0.0 1552.9 jit_solution(1215625916999225624)
XLA Ops:
  8.0 14.9 all-gather.1
  23.0 12.2 all-gather
  38.9 43.6 %all-gather.10.cloned.1.call-done = bf16[768,2304]{1,0:T(8,128)(2,1)} async-done(((bf16[192,2304]{1,0:T(8,128)(2,1)}), bf16[768,2304]{1,0:T(8,128)(2,1)}) %all-gather.10.cloned.1.call-update) | async-done | bytes 3538960 | tf_op jit(solution)/shard_map/all_gather | solution.py:82
  94.3 20.7 %collective-permute-done = bf16[512,768]{1,0:T(8,128)(2,1)S(1)} collective-permute-done((bf16[512,768]{1,0:T(8,128)(2,1)S(1)}, bf16[512,768]{1,0:T(8,128)(2,1)S(1)}, u32[]{:S(2)}, u32[]{:S(2)}) %collective-permute-start) | collective-permute-done | bytes 786464 | tf_op jit(solution)/shard_map/ppermute | solution.py:114
  115.0 26.0 %collective-permute-done.1 = bf16[512,768]{1,0:T(8,128)(2,1)S(1)} collective-permute-done((bf16[512,768]{1,0:T(8,128)(2,1)S(1)}, bf16[512,768]{1,0:T(8,128)(2,1)S(1)}, u32[]{:S(2)}, u32[]{:S(2)}) %collective-permute-start.1) | collective-permute-done | bytes 786464 | tf_op jit(solution)/shard_map/ppermute | solution.py:114
  141.0 12.3 collective-permute-done.2
  153.3 12.4 collective-permute-done.3
  166.1 12.2 collective-permute-done.4
  178.5 13.2 all-gather.2
  192.4 13.3 all_gather.43
  208.0 10.5 collective-permute-done.6
  272.8 179.6 %while.30 = (s32[]{:T(128)}, f32[12,512]{1,0:T(8,128)S(1)}, f32[12,512]{1,0:T(8,128)S(1)}, f32[12,512,64]{1,2,0:T(8,128)}, s32[8,512]{1,0:T(8,128)S(1)}, /*index...) while((s32[]{:T(128)}, f32[12,512]{1,0:T(8,128)S(1)}, ...), condition=%wide.region_10.11_spmd.clone, body=%wide.region_7.10_spmd.clone.sunk | while | flops 848197632 | bytes 95043760 | solution.py:146
  460.4 21.6 %fusion.101 = (f32[512]{0:T(512)S(1)}, f32[512,3072]{1,0:T(8,128)}, f32[512,3072]{1,0:T(8,128)}, f32[512,3072]{1,0:T(8,128)}) fusion(f32[3072]{0:T(1024)S(1)} %bitcast.270, bf16[768,3072]{1,0:T(8,128)(2,1)} %all-gather.16.cloned.1.call-done, f32[512,768]{1,0:T(8,128)} %copy-done.13, f32[768]{0:T(1024)S(1)} %get-tuple-element.371, ...), kind=kOutput, calls=%fused_computation.222 | convolution fusion | flops 2521693696 | bytes 25190400 | tf_op jit(solution)/shard_map/dot_general | solution.py:156
  492.7 8.9 copy.99
  513.7 11.4 convert_reduce_fusion
  539.4 251.5 %while.31 = (s32[]{:T(128)}, f32[512,12,64]{0,2,1:T(8,128)}, bf16[8,512,12,64]{1,3,2,0:T(8,128)(2,1)}, bf16[8,512,12,64]{1,3,2,0:T(8,128)(2,1)}, bf16[8,512,12,6...) while((s32[]{:T(128)}, f32[512,12,64]{0,2,1:T(8,128)}, ...), condition=%wide.region_24.25_spmd.clone, body=%wide.region_23.24_spmd.clone.sunk | while | flops 2047082496 | bytes 195125520 | solution.py:255
  842.0 24.1 %reduce-scatter.14.cloned.1.call-done = bf16[512,768]{0,1:T(8,128)(2,1)} async-done(((bf16[4096,768]{0,1:T(8,128)(2,1)}), bf16[512,768]{0,1:T(8,128)(2,1)}) %reduce-scatter.14.cloned.1.call-update) | async-done | bytes 786448 | tf_op jit(solution)/shard_map/reduce_scatter | solution.py:271
  866.1 65.5 %reduce-scatter.12.cloned.1.call-done = bf16[512,768]{0,1:T(8,128)(2,1)} async-done(((bf16[4096,768]{0,1:T(8,128)(2,1)}), bf16[512,768]{0,1:T(8,128)(2,1)}) %reduce-scatter.12.cloned.1.call-update) | async-done | bytes 786448 | tf_op jit(solution)/shard_map/reduce_scatter | solution.py:268
  946.5 87.5 %reduce-scatter.24.cloned.1.call-done = f32[96,2]{1,0:T(8,128)} async-done(((f32[3072,2]{1,0:T(8,128)}), f32[96,2]{1,0:T(8,128)}) %reduce-scatter.24.cloned.1.call-update) | async-done | bytes 784
  1043.7 40.8 %all-reduce.3 = (f32[3,768]{1,0:T(4,128)S(1)}, f32[7,768]{1,0:T(8,128)S(1)}, f32[3072]{0:T(1024)S(1)}) all-reduce(f32[3,768]{1,0:T(4,128)S(1)} %pad_maximum_fusion.2, f32[7,768]{1,0:T(8,128)S(1)} %stack.36, f32[3072]{0:T(1024)S(1)} %copy-done.31), channel_id=8, replica_groups=mesh['ctx'=8,'fsdp'=4] {'ctx','fsdp'}, use_global_device_ids=true, to_apply=%region_36.37.clone | all-reduce | flops 10752 | bytes 86016
  1086.5 51.3 %reduce-scatter.18.cloned.1.call-done = f32[24,768]{1,0:T(8,128)} async-done(((f32[768,768]{1,0:T(8,128)}), f32[24,768]{1,0:T(8,128)}) %reduce-scatter.18.cloned.1.call-update) | async-done | bytes 73744 | tf_op jit(solution)/shard_map/reduce_scatter | solution.py:301
  1137.7 142.2 %reduce-scatter.20.cloned.1.call-done = f32[24,3072]{1,0:T(8,128)} async-done(((f32[768,3072]{1,0:T(8,128)}), f32[24,3072]{1,0:T(8,128)}) %reduce-scatter.20.cloned.1.call-update) | async-done | bytes 294928 | tf_op jit(solution)/shard_map/reduce_scatter | solution.py:302
  1279.9 140.8 %reduce-scatter.22.cloned.1.call-done = f32[96,768]{1,0:T(8,128)} async-done(((f32[3072,768]{1,0:T(8,128)}), f32[96,768]{1,0:T(8,128)}) %reduce-scatter.22.cloned.1.call-update) | async-done | bytes 294928 | tf_op jit(solution)/shard_map/reduce_scatter | solution.py:303
  1420.8 125.3 %reduce-scatter.16.cloned.1.call-done = f32[24,2304]{1,0:T(8,128)} async-done(((f32[768,2304]{1,0:T(8,128)}), f32[24,2304]{1,0:T(8,128)}) %reduce-scatter.16.cloned.1.call-update) | async-done | bytes 221200 | tf_op jit(solution)/shard_map/reduce_scatter | solution.py:300
  (462 shorter events, 625.0 us)
Async XLA Ops:
  7.2 75.3 %all-gather.10.cloned.1.call-start = ((), (), s32[]{:S(2)}) async-start(), calls=%async_computation.7 | async-start | bytes 4423680 | tf_op jit(solution)/shard_map/all_gather | solution.py:82
  7.9 244.3 %all-gather.12.cloned.1.call-start = ((), (), s32[]{:S(2)}) async-start(), calls=%async_computation.8 | async-start | bytes 7077888 | tf_op jit(solution)/shard_map/all_gather | solution.py:110
  36.0 420.1 %copy-start.49 = (f32[768]{0:T(1024)}, f32[768]{0:T(1024)S(1)}, u32[]{:S(2)}) copy-start(f32[768]{0:T(1024)S(1)} %get-tuple-element.373) | copy-start | bytes 9220
  36.0 424.4 %copy-start.47 = (f32[768]{0:T(1024)}, f32[768]{0:T(1024)S(1)}, u32[]{:S(2)}) copy-start(f32[768]{0:T(1024)S(1)} %get-tuple-element.371) | copy-start | bytes 9220
  89.1 103.2 %copy-start.55 = (bf16[2,768]{1,0:T(2,128)(2,1)S(1)}, bf16[2,768]{1,0:T(2,128)(2,1)}, u32[]{:S(2)}) copy-start(bf16[2,768]{1,0:T(2,128)(2,1)} %param.27) | copy-start | bytes 9220
  90.1 366.0 %all-gather.14.cloned.1.call-start = ((), (), s32[]{:S(2)}) async-start(), calls=%async_computation.9 | async-start | bytes 1474560 | tf_op jit(solution)/shard_map/all_gather | solution.py:83
  90.8 369.5 %all-gather.16.cloned.1.call-start = ((), (), s32[]{:S(2)}) async-start(), calls=%async_computation.10 | async-start | bytes 5898240 | tf_op jit(solution)/shard_map/all_gather | solution.py:84
  91.4 390.6 %all-gather.18.cloned.1.call-start = ((), (), s32[]{:S(2)}) async-start(), calls=%async_computation.11 | async-start | bytes 5898240 | tf_op jit(solution)/shard_map/all_gather | solution.py:85
  92.0 400.7 %all-gather.20.cloned.1.call-start = ((), (), s32[]{:S(2)}) async-start(), calls=%async_computation.12 | async-start | bytes 7077888 | tf_op jit(solution)/shard_map/all_gather | solution.py:243
  94.2 113.6 %copy-start.9 = (bf16[512,768]{1,0:T(8,128)(2,1)}, bf16[512,768]{1,0:T(8,128)(2,1)S(1)}, u32[]{:S(2)}) copy-start(bf16[512,768]{1,0:T(8,128)(2,1)S(1)} %get-tuple-element.455) | copy-start | bytes 2359300
  94.2 20.8 %collective-permute-start = (bf16[512,768]{1,0:T(8,128)(2,1)S(1)}, bf16[512,768]{1,0:T(8,128)(2,1)S(1)}, u32[]{:S(2)}, u32[]{:S(2)}) collective-permute-start(bf16[512,768]{1,0:T(8,128)(2,1)S(1)} %get-tuple-element.455), channel_id=1, source_target_pairs={{0,4},{4,8},{8,12},{12,16},{16,20},{20,24},{24,28},{28,0},{1,5},{5... | collective-permute-start | bytes 2359304 | tf_op jit(solution)/shard_map/ppermute | solution.py:114
  115.0 26.0 %collective-permute-start.1 = (bf16[512,768]{1,0:T(8,128)(2,1)S(1)}, bf16[512,768]{1,0:T(8,128)(2,1)S(1)}, u32[]{:S(2)}, u32[]{:S(2)}) collective-permute-start(bf16[512,768]{1,0:T(8,128)(2,1)S(1)} %collective-permute-done), channel_id=1, source_target_pairs={{0,4},{4,8},{8,12},{12,16},{16,20},{20,24},{24,28},{28,0},{1,5},{5... | collective-permute-start | bytes 2359304 | tf_op jit(solution)/shard_map/ppermute | solution.py:114
  141.0 12.3 collective-permute-start.2
  153.3 12.4 collective-permute-start.3
  165.7 12.6 collective-permute-start.4
  178.3 27.5 %collective-permute-start.5 = (bf16[512,768]{1,0:T(8,128)(2,1)}, bf16[512,768]{1,0:T(8,128)(2,1)}, u32[]{:S(2)}, u32[]{:S(2)}) collective-permute-start(bf16[512,768]{1,0:T(8,128)(2,1)} %collective-permute-done.4), channel_id=1, source_target_pairs={{0,4},{4,8},{8,12},{12,16},{16,20},{20,24},{24,28},{28,0},{1,5},{5... | collective-permute-start | bytes 2359304 | tf_op jit(solution)/shard_map/ppermute | solution.py:114
  205.8 12.7 collective-permute-start.6
  207.8 658.3 %reduce-scatter.14.cloned.1.call-start = ((), (), s32[]{:S(2)}) async-start(), calls=%async_computation.14 | async-start | bytes 7077888 | tf_op jit(solution)/shard_map/reduce_scatter | solution.py:271
  804.8 126.9 %reduce-scatter.12.cloned.1.call-start = ((), (), s32[]{:S(2)}) async-start(), calls=%async_computation.13 | async-start | bytes 7077888 | tf_op jit(solution)/shard_map/reduce_scatter | solution.py:268
  819.0 215.0 %reduce-scatter.24.cloned.1.call-start = ((), (), s32[]{:S(2)}) async-start(), calls=%async_computation.19 | async-start | bytes 1622016
  821.4 316.4 %reduce-scatter.18.cloned.1.call-start = ((), (), s32[]{:S(2)}) async-start(), calls=%async_computation.16 | async-start | bytes 2433024 | tf_op jit(solution)/shard_map/reduce_scatter | solution.py:301
  825.0 454.9 %reduce-scatter.20.cloned.1.call-start = ((), (), s32[]{:S(2)}) async-start(), calls=%async_computation.17 | async-start | bytes 9732096 | tf_op jit(solution)/shard_map/reduce_scatter | solution.py:302
  832.3 588.4 %reduce-scatter.22.cloned.1.call-start = ((), (), s32[]{:S(2)}) async-start(), calls=%async_computation.18 | async-start | bytes 9732096 | tf_op jit(solution)/shard_map/reduce_scatter | solution.py:303
  840.5 705.6 %reduce-scatter.16.cloned.1.call-start = ((), (), s32[]{:S(2)}) async-start(), calls=%async_computation.15 | async-start | bytes 7299072 | tf_op jit(solution)/shard_map/reduce_scatter | solution.py:300
  (86 other events, 1407.1 us)
Sparse Core Ops, SparseCore 0:
  9.6 72.8 all-gather.9
  90.2 55.7 all-gather.11
  147.6 29.3 all-gather.13
  178.4 88.6 all-gather.15
  268.5 87.8 all-gather.17
  358.2 43.9 all-gather.19
  804.9 61.1 reduce-scatter.13
  869.9 61.7 reduce-scatter.11
  936.9 97.0 reduce-scatter.23
  1039.7 98.0 reduce-scatter.17
  1145.2 134.6 reduce-scatter.19
  1286.3 134.4 reduce-scatter.21
  1428.0 118.0 reduce-scatter.15
